TPU v7x, 256 devices: a whole 4x4x8 slice. The times are simulated.
256 devices in a mesh: samp: 16 (over z_hi, x, core), gene: 4 (over z_lo), snp: 4 (over y).
Axes of the slice: x: 4, y: 4, z: 8 (z_hi: 2, z_lo: 4; z = z_hi * 4 + z_lo), core: 2. Of those that a mesh axis runs over, the one named last changes fastest.
Arguments:
- expression: bfloat16 [4096, 16384], P('samp', ('gene', 'snp')), may hold values from -6 to 6
- loadings: bfloat16 [16384, 128], P(('gene', 'snp')), may hold values from -0.046875 to 0.046875
- dosage: bfloat16 [4096, 16384], P(None, ('gene', 'snp')), may hold values from 0 to 2
Outputs:
- assoc: bfloat16 [16, 16, 64, 16384], P(None, 'samp', None, ('gene', 'snp'))
All inputs are finite; a program needn't handle non-finite values.
Results may differ from a plain program's by a relative error of at most 0.0065.
Values may be sent and summed in bfloat16 or wider, within the bound.
No kernel may reach another device: no remote copies, remote signals or barrier semaphores. Data moves between devices by JAX's collectives and lax.ppermute only.
A program may use at most 64 MiB of HBM per device.

v0:
```python
import jax
import jax.numpy as jnp
from jax import lax
from jax.sharding import PartitionSpec as P

ridge_factor = 1.0
ridge_sample = 1.0


def body(expression, loadings, dosage):
    contract = (((0,), (0,)), ((), ()))
    factor_count = loadings.shape[1]
    identity = jnp.eye(factor_count, dtype=jnp.float32)
    panel_genes = expression.shape[1] // lax.axis_size("samp")
    all_samples = dosage.shape[0]
    snp_count = dosage.shape[1]
    block_count = lax.axis_size("gene") * lax.axis_size("snp")
    norm_scale = 1.0 / jnp.sqrt(jnp.float32(all_samples))
    local_factor = jnp.dot(expression, loadings, preferred_element_type=jnp.float32)
    local_gram = lax.dot_general(loadings, loadings, contract, preferred_element_type=jnp.float32)
    factor_sum, gram_sum = lax.psum((local_factor, local_gram), ("gene", "snp"))
    lower_gram = jnp.linalg.cholesky(gram_sum + ridge_factor * identity)
    factors = jax.scipy.linalg.cho_solve((lower_gram, True), factor_sum.T).T.astype(jnp.bfloat16)
    local_hess = lax.dot_general(factors, factors, contract, preferred_element_type=jnp.float32)
    local_cross = lax.dot_general(factors, expression, contract, preferred_element_type=jnp.float32)
    hess_sum, cross_sum = lax.psum((local_hess, local_cross), "samp")
    lower_hess = jnp.linalg.cholesky(hess_sum + ridge_sample * identity)
    fit_coef = jax.scipy.linalg.cho_solve((lower_hess, True), cross_sum).astype(jnp.bfloat16)
    fitted = lax.dot_general(
        fit_coef, factors, (((0,), (1,)), ((), ())), preferred_element_type=jnp.float32
    )
    residual_t = (expression.T.astype(jnp.float32) - fitted).astype(jnp.bfloat16)
    panel_resid = lax.all_to_all(residual_t, "samp", split_axis=0, concat_axis=1, tiled=True)
    totals = (
        jnp.dot(
            lax.all_gather(panel_resid, ("gene", "snp"), axis=0, tiled=True),
            dosage,
            preferred_element_type=jnp.float32,
        )
        * norm_scale
    )
    return totals.astype(jnp.bfloat16).reshape(block_count, 1, panel_genes, snp_count)


def solution(mesh):
    placed = (P("samp", ("gene", "snp")), P(("gene", "snp"), None), P(None, ("gene", "snp")))
    return jax.shard_map(
        body,
        mesh=mesh,
        in_specs=placed,
        out_specs=P(None, "samp", None, ("gene", "snp")),
        check_vma=False,
    )
```

profile of v0, /device:TPU:1, one launch (start us, length us, event | category | flops | bytes accessed | tf_op | source)
XLA Modules:
  0.0 548.4 jit_solution(741673774838986686)
XLA Ops:
  6.5 0.9 copy-done
  7.5 0.9 fusion.13
  8.4 2.0 fusion.14
  10.4 148.5 %all-reduce.5.cloned.1.call-done = (f32[256,128]{1,0:T(8,128)}, f32[128,128]{0,1:T(8,128)}) async-done(((f32[256,128]{1,0:T(8,128)}, f32[128,128]{0,1:T(8,128)}), (f32[256,128]{1,0:T(8,128)}, f32[128,128]{0,1:T(8,128)})) %all-reduce.5.cloned.1.call-update) | async-done | bytes 196624 | tf_op jit(solution)/shard_map/psum | solution.py:21
  159.0 0.9 convert_add_fusion.1
  159.8 0.1 copy.19
  159.9 0.9 fusion.10
  160.8 11.7 %cholesky.44 = f32[128,128]{1,0:T(8,128)S(1)} custom-call(f32[128,128]{1,0:T(8,128)S(1)} %fusion.10), custom_call_target="Cholesky" | custom-call | tf_op jit(solution)/shard_map/jit(cholesky)/cholesky | solution.py:22
  172.5 0.6 compare_reduce_fusion.1
  173.2 0.7 fusion.1
  173.8 9.8 %custom-call.16 = f32[1,128,128]{1,2,0:T(8,128)S(1)} custom-call(f32[1,128,128]{2,1,0:T(8,128)S(1)} %fusion.1), custom_call_target="InvertDiagBlocksLowerTriangular" | custom-call | tf_op jit(solution)/shard_map/jit(_cho_solve)/triangular_solve | solution.py:23
  183.6 1.2 fusion.8
  184.9 0.4 convolution_convert_fusion.1
  185.3 0.8 fusion.15
  186.1 2.1 fusion.16
  188.2 0.2 all-gather.2.cloned.1.call-start
  188.4 1.2 copy.17
  189.7 183.0 %all-reduce.7.cloned.1.call-done = (f32[128,1024]{1,0:T(8,128)}, f32[128,128]{0,1:T(8,128)}) async-done(((f32[128,1024]{1,0:T(8,128)}, f32[128,128]{0,1:T(8,128)}), (f32[128,1024]{1,0:T(8,128)}, f32[128,128]{0,1:T(8,128)})) %all-reduce.7.cloned.1.call-update) | async-done | bytes 589840 | tf_op jit(solution)/shard_map/psum | solution.py:26
  372.7 0.9 convert_add_fusion
  373.5 0.1 copy.21
  373.6 0.9 fusion.6
  374.5 11.7 %cholesky.55 = f32[128,128]{1,0:T(8,128)S(1)} custom-call(f32[128,128]{1,0:T(8,128)S(1)} %fusion.6), custom_call_target="Cholesky" | custom-call | tf_op jit(solution)/shard_map/jit(cholesky)/cholesky | solution.py:27
  386.3 0.6 compare_reduce_fusion
  386.9 0.7 fusion.2
  387.6 9.8 %custom-call.17 = f32[1,128,128]{1,2,0:T(8,128)S(1)} custom-call(f32[1,128,128]{2,1,0:T(8,128)S(1)} %fusion.2), custom_call_target="InvertDiagBlocksLowerTriangular" | custom-call | tf_op jit(solution)/shard_map/jit(_cho_solve)/triangular_solve | solution.py:28
  397.4 1.7 fusion.4
  399.0 0.6 convolution_convert_fusion
  399.6 0.3 fusion
  400.0 21.6 %all_to_all.19 = bf16[16,64,256]{2,1,0:T(8,128)(2,1)S(1)} all-to-all(bf16[16,64,256]{2,1,0:T(8,128)(2,1)S(1)} %bitcast.48), channel_id=1, replica_groups=mesh['samp'=16,'gene'=4,'snp'=4] {'samp'}, dimensions={0} | all-to-all | bytes 1048576 | tf_op jit(solution)/shard_map/all_to_all | solution.py:33
  421.6 0.8 copy.26
  422.5 104.8 %all-gather.2.cloned.1.call-done = bf16[1024,4096]{1,0:T(8,128)(2,1)} async-done(((bf16[64,4096]{1,0:T(8,128)(2,1)}), bf16[1024,4096]{1,0:T(8,128)(2,1)}) %all-gather.2.cloned.1.call-update) | async-done | bytes 8388624 | tf_op jit(solution)/shard_map/all_gather | solution.py:36
  527.3 14.6 %multiply_convert_fusion = bf16[1024,1024]{1,0:T(8,128)(2,1)} fusion(bf16[1024,4096]{1,0:T(8,128)(2,1)} %all-gather.2.cloned.1.call-done, bf16[4096,1024]{1,0:T(8,128)(2,1)} %param.6), kind=kOutput, calls=%fused_computation | convolution fusion | flops 8592031744 | bytes 18874368 | tf_op jit(solution)/shard_map/dot_general | solution.py:35
  (8 shorter events, 0.2 us)
Async XLA Ops:
  6.5 1.0 copy-start
  6.5 152.4 %all-reduce.5.cloned.1.call-start = ((), (), s32[]{:S(2)}) async-start(), calls=%async_computation.2 | async-start | bytes 393216 | tf_op jit(solution)/shard_map/psum | solution.py:21
  10.4 362.3 %all-reduce.7.cloned.1.call-start = ((), (), s32[]{:S(2)}) async-start(), calls=%async_computation.3 | async-start | bytes 1179648 | tf_op jit(solution)/shard_map/psum | solution.py:26
  188.2 339.1 %all-gather.2.cloned.1.call-start = ((), (), s32[]{:S(2)}) async-start(), calls=%async_computation.1 | async-start | bytes 8912896 | tf_op jit(solution)/shard_map/all_gather | solution.py:36
Sparse Core Ops, SparseCore 0:
  10.5 148.4 all-reduce.4
  188.3 184.3 all-reduce.6
  422.6 104.6 all-gather.1
where the time goes:
time: 549 us; the launch traced here: 548 us
  waiting for transfers between devices  436 us (79%)
  other arithmetic  49.1 us (9%)
  matrix products  24.6 us (4%)
  blocking collectives  21.6 us (4%)
  between operations  13.2 us (2%)
    psum x1, waiting for transfers between devices, body(): hess_sum, cross_sum = lax.psum((local_hess, local_cross), 'samp')  183 us
    psum x1, waiting for transfers between devices, body(): factor_sum, gram_sum = lax.psum((local_factor, local_gram), ('gene', 'snp'))  149 us
    all_gather x1, waiting for transfers between devices, body(): lax.all_gather(panel_resid, ('gene', 'snp'), axis=0, tiled=True)  105 us
    all_to_all x1, blocking collectives, body(): lax.all_to_all(residual_t, 'samp', split_axis=0, concat_axis=1, tiled=True)  21.6 us
    dot_general x1, matrix products, body(): jnp.dot(lax.all_gather(panel_resid, ('gene', 'snp'), axis=0, tiled=True),...  14.6 us
    another operation x3, other arithmetic, body(): lower_hess = jnp.linalg.cholesky(hess_sum + ridge_sample * identity)  12.4 us
    another operation x3, other arithmetic, body(): lower_gram = jnp.linalg.cholesky(gram_sum + ridge_factor * identity)  12.4 us
  transfers between devices with their start and end apart: 3, of which 3 were waited for; matrix products, arithmetic and copies ran while one was open for 0% of the time, Pallas kernels for 0%

commit v1 on v0

--- a/solution.py
+++ b/solution.py
@@ -5,6 +5,12 @@
 
 ridge_factor = 1.0
 ridge_sample = 1.0
+
+
+def get_series(x_part):
+    for src_i in ("snp", "gene"):
+        x_part = lax.psum(x_part, src_i)
+    return x_part
 
 
 def body(expression, loadings, dosage):
@@ -18,7 +24,7 @@
     norm_scale = 1.0 / jnp.sqrt(jnp.float32(all_samples))
     local_factor = jnp.dot(expression, loadings, preferred_element_type=jnp.float32)
     local_gram = lax.dot_general(loadings, loadings, contract, preferred_element_type=jnp.float32)
-    factor_sum, gram_sum = lax.psum((local_factor, local_gram), ("gene", "snp"))
+    factor_sum, gram_sum = get_series((local_factor, local_gram))
     lower_gram = jnp.linalg.cholesky(gram_sum + ridge_factor * identity)
     factors = jax.scipy.linalg.cho_solve((lower_gram, True), factor_sum.T).T.astype(jnp.bfloat16)
     local_hess = lax.dot_general(factors, factors, contract, preferred_element_type=jnp.float32)

time: 549 us -> 493 us (0.90)
  waiting for transfers between devices: 436 us -> 381 us
    psum x1 -> x2, waiting for transfers between devices: 149 us -> 101 us  [get_series(): x_part = lax.psum(x_part, src_i)]
    psum x1, waiting for transfers between devices: 183 us -> 175 us  [body(): hess_sum, cross_sum = lax.psum((local_hess, local_cross), 'samp')]
  transfers between devices with their start and end apart: 3 -> 4, of which waited for: 3 -> 4; matrix products, arithmetic and copies ran while one was open for 0% -> 0% of each run, Pallas kernels for 0% -> 0%
where the time goes in v1:
time: 493 us
  waiting for transfers between devices  381 us (77%)
  other arithmetic  49.1 us (10%)
  matrix products  24.6 us (5%)
  blocking collectives  21.6 us (4%)
  between operations  13.2 us (3%)
    psum x1, waiting for transfers between devices, body(): hess_sum, cross_sum = lax.psum((local_hess, local_cross), 'samp')  175 us
    all_gather x1, waiting for transfers between devices, body(): lax.all_gather(panel_resid, ('gene', 'snp'), axis=0, tiled=True)  105 us
    psum x2, waiting for transfers between devices, get_series(): x_part = lax.psum(x_part, src_i)  101 us
    all_to_all x1, blocking collectives, body(): lax.all_to_all(residual_t, 'samp', split_axis=0, concat_axis=1, tiled=True)  21.6 us
    dot_general x1, matrix products, body(): jnp.dot(lax.all_gather(panel_resid, ('gene', 'snp'), axis=0, tiled=True),...  14.6 us
    another operation x3, other arithmetic, body(): lower_gram = jnp.linalg.cholesky(gram_sum + ridge_factor * identity)  12.4 us
    another operation x3, other arithmetic, body(): lower_hess = jnp.linalg.cholesky(hess_sum + ridge_sample * identity)  12.4 us
    another operation x2, other arithmetic, body(): jax.scipy.linalg.cho_solve((lower_gram, True), factor_sum.T)  10.5 us
  transfers between devices with their start and end apart: 4, of which 4 were waited for; matrix products, arithmetic and copies ran while one was open for 0% of the time, Pallas kernels for 0%

profile of v1, /device:TPU:1, one launch (start us, length us, event | category | flops | bytes accessed | tf_op | source)
XLA Modules:
  0.0 492.8 jit_solution(3611915984451497624)
XLA Ops:
  6.5 0.9 copy-done
  7.5 0.9 fusion.13
  8.4 2.0 fusion.14
  10.4 48.6 %all-reduce.9.cloned.1.call-done = (f32[256,128]{1,0:T(8,128)}, f32[128,128]{0,1:T(8,128)}) async-done(((f32[256,128]{1,0:T(8,128)}, f32[128,128]{0,1:T(8,128)}), (f32[256,128]{1,0:T(8,128)}, f32[128,128]{0,1:T(8,128)})) %all-reduce.9.cloned.1.call-update) | async-done | bytes 196624 | tf_op jit(solution)/shard_map/psum | solution.py:12
  59.1 52.3 %all-reduce.11.cloned.1.call-done = (f32[256,128]{1,0:T(8,128)}, f32[128,128]{0,1:T(8,128)}) async-done(((f32[256,128]{1,0:T(8,128)}, f32[128,128]{0,1:T(8,128)}), (f32[256,128]{1,0:T(8,128)}, f32[128,128]{0,1:T(8,128)})) %all-reduce.11.cloned.1.call-update) | async-done | bytes 196624 | tf_op jit(solution)/shard_map/psum | solution.py:12
  111.4 0.9 convert_add_fusion.1
  112.2 0.1 copy.19
  112.3 0.9 fusion.10
  113.2 11.7 %cholesky.44 = f32[128,128]{1,0:T(8,128)S(1)} custom-call(f32[128,128]{1,0:T(8,128)S(1)} %fusion.10), custom_call_target="Cholesky" | custom-call | tf_op jit(solution)/shard_map/jit(cholesky)/cholesky | solution.py:28
  124.9 0.6 compare_reduce_fusion.1
  125.6 0.7 fusion.1
  126.2 9.8 %custom-call.16 = f32[1,128,128]{1,2,0:T(8,128)S(1)} custom-call(f32[1,128,128]{2,1,0:T(8,128)S(1)} %fusion.1), custom_call_target="InvertDiagBlocksLowerTriangular" | custom-call | tf_op jit(solution)/shard_map/jit(_cho_solve)/triangular_solve | solution.py:29
  136.1 1.2 fusion.8
  137.3 0.4 convolution_convert_fusion.1
  137.7 0.8 fusion.15
  138.5 2.1 fusion.16
  140.6 0.2 all-gather.2.cloned.1.call-start
  140.9 1.2 copy.17
  142.1 175.0 %all-reduce.7.cloned.1.call-done = (f32[128,1024]{1,0:T(8,128)}, f32[128,128]{0,1:T(8,128)}) async-done(((f32[128,1024]{1,0:T(8,128)}, f32[128,128]{0,1:T(8,128)}), (f32[128,1024]{1,0:T(8,128)}, f32[128,128]{0,1:T(8,128)})) %all-reduce.7.cloned.1.call-update) | async-done | bytes 589840 | tf_op jit(solution)/shard_map/psum | solution.py:32
  317.1 0.9 convert_add_fusion
  318.0 0.9 fusion.6
  318.9 11.7 %cholesky.55 = f32[128,128]{1,0:T(8,128)S(1)} custom-call(f32[128,128]{1,0:T(8,128)S(1)} %fusion.6), custom_call_target="Cholesky" | custom-call | tf_op jit(solution)/shard_map/jit(cholesky)/cholesky | solution.py:33
  330.6 0.6 compare_reduce_fusion
  331.3 0.7 fusion.2
  331.9 9.8 %custom-call.17 = f32[1,128,128]{1,2,0:T(8,128)S(1)} custom-call(f32[1,128,128]{2,1,0:T(8,128)S(1)} %fusion.2), custom_call_target="InvertDiagBlocksLowerTriangular" | custom-call | tf_op jit(solution)/shard_map/jit(_cho_solve)/triangular_solve | solution.py:34
  341.8 1.7 fusion.4
  343.4 0.6 convolution_convert_fusion
  344.0 0.3 fusion
  344.4 21.6 %all_to_all.19 = bf16[16,64,256]{2,1,0:T(8,128)(2,1)S(1)} all-to-all(bf16[16,64,256]{2,1,0:T(8,128)(2,1)S(1)} %bitcast.48), channel_id=1, replica_groups=mesh['samp'=16,'gene'=4,'snp'=4] {'samp'}, dimensions={0} | all-to-all | bytes 1048576 | tf_op jit(solution)/shard_map/all_to_all | solution.py:39
  366.0 0.8 copy.26
  366.8 104.8 %all-gather.2.cloned.1.call-done = bf16[1024,4096]{1,0:T(8,128)(2,1)} async-done(((bf16[64,4096]{1,0:T(8,128)(2,1)}), bf16[1024,4096]{1,0:T(8,128)(2,1)}) %all-gather.2.cloned.1.call-update) | async-done | bytes 8388624 | tf_op jit(solution)/shard_map/all_gather | solution.py:42
  471.7 14.6 %multiply_convert_fusion = bf16[1024,1024]{1,0:T(8,128)(2,1)} fusion(bf16[1024,4096]{1,0:T(8,128)(2,1)} %all-gather.2.cloned.1.call-done, bf16[4096,1024]{1,0:T(8,128)(2,1)} %param.6), kind=kOutput, calls=%fused_computation | convolution fusion | flops 8592031744 | bytes 18874368 | tf_op jit(solution)/shard_map/dot_general | solution.py:41
  (11 shorter events, 0.3 us)
Async XLA Ops:
  6.5 1.0 copy-start
  6.5 52.5 %all-reduce.9.cloned.1.call-start = ((), (), s32[]{:S(2)}) async-start(), calls=%async_computation.3 | async-start | bytes 393216 | tf_op jit(solution)/shard_map/psum | solution.py:12
  10.4 101.0 %all-reduce.11.cloned.1.call-start = ((), (), s32[]{:S(2)}) async-start(), calls=%async_computation.4 | async-start | bytes 393216 | tf_op jit(solution)/shard_map/psum | solution.py:12
  59.0 258.0 %all-reduce.7.cloned.1.call-start = ((), (), s32[]{:S(2)}) async-start(), calls=%async_computation.2 | async-start | bytes 1179648 | tf_op jit(solution)/shard_map/psum | solution.py:32
  140.6 331.0 %all-gather.2.cloned.1.call-start = ((), (), s32[]{:S(2)}) async-start(), calls=%async_computation.1 | async-start | bytes 8912896 | tf_op jit(solution)/shard_map/all_gather | solution.py:42
Sparse Core Ops, SparseCore 0:
  10.5 48.4 all-reduce.8
  61.7 49.6 all-reduce.10
  140.7 176.2 all-reduce.6
  367.0 104.6 all-gather.1

commit v2 on v0

--- a/solution.py
+++ b/solution.py
@@ -1,10 +1,21 @@
+import functools
 import jax
 import jax.numpy as jnp
 from jax import lax
 from jax.sharding import PartitionSpec as P
+from jax.lax import all_to_all, axis_size
 
 ridge_factor = 1.0
 ridge_sample = 1.0
+
+
+def set_islands_by_axis(mine_x, dim_i):
+    field_out = jnp.stack([mine_x for _ in range(axis_size(("gene", "snp")))])
+    w_next = all_to_all(field_out, ("gene", "snp"), 0, 0)
+    return jnp.concatenate(w_next, dim_i)
+
+
+read_results = functools.partial(set_islands_by_axis, dim_i=0)
 
 
 def body(expression, loadings, dosage):
@@ -32,12 +43,7 @@
     residual_t = (expression.T.astype(jnp.float32) - fitted).astype(jnp.bfloat16)
     panel_resid = lax.all_to_all(residual_t, "samp", split_axis=0, concat_axis=1, tiled=True)
     totals = (
-        jnp.dot(
-            lax.all_gather(panel_resid, ("gene", "snp"), axis=0, tiled=True),
-            dosage,
-            preferred_element_type=jnp.float32,
-        )
-        * norm_scale
+        jnp.dot(read_results(panel_resid), dosage, preferred_element_type=jnp.float32) * norm_scale
     )
     return totals.astype(jnp.bfloat16).reshape(block_count, 1, panel_genes, snp_count)
 

time: 549 us -> 635 us (1.16)
  blocking collectives: 21.6 us -> 216 us
  waiting for transfers between devices: 436 us -> 332 us
    all_to_all x0 -> x1, blocking collectives: none -> 194 us  [set_islands_by_axis(): w_next = all_to_all(field_out, ('gene', 'snp'), 0, 0)]
    all_gather x1 -> x0, waiting for transfers between devices: 105 us -> none  [body(): lax.all_gather(panel_resid, ('gene', 'snp'), axis=0, tiled=True)]
  transfers between devices with their start and end apart: 3 -> 2, of which waited for: 3 -> 2; matrix products, arithmetic and copies ran while one was open for 0% -> 0% of each run, Pallas kernels for 0% -> 0%
where the time goes in v2:
time: 635 us; the launch traced here: 634 us
  waiting for transfers between devices  332 us (52%)
  blocking collectives  216 us (34%)
  other arithmetic  49.3 us (8%)
  matrix products  20 us (3%)
  between operations  13.5 us (2%)
    all_to_all x1, blocking collectives, set_islands_by_axis(): w_next = all_to_all(field_out, ('gene', 'snp'), 0, 0)  194 us
    psum x1, waiting for transfers between devices, body(): hess_sum, cross_sum = lax.psum((local_hess, local_cross), 'samp')  183 us
    psum x1, waiting for transfers between devices, body(): factor_sum, gram_sum = lax.psum((local_factor, local_gram), ('gene', 'snp'))  149 us
    all_to_all x1, blocking collectives, body(): lax.all_to_all(residual_t, 'samp', split_axis=0, concat_axis=1, tiled=True)  21.6 us
  transfers between devices with their start and end apart: 2, of which 2 were waited for; matrix products, arithmetic and copies ran while one was open for 0% of the time, Pallas kernels for 0%

profile of v2, /device:TPU:1, one launch (start us, length us, event | category | flops | bytes accessed | tf_op | source)
XLA Modules:
  0.0 634.2 jit_solution(14797989725246243701)
XLA Ops:
  6.5 0.9 copy-done
  7.5 0.9 fusion.13
  8.4 2.0 fusion.14
  10.4 0.0 all-reduce.7.cloned.1.call-start
  10.4 148.5 %all-reduce.5.cloned.1.call-done = (f32[256,128]{1,0:T(8,128)}, f32[128,128]{0,1:T(8,128)}) async-done(((f32[256,128]{1,0:T(8,128)}, f32[128,128]{0,1:T(8,128)}), (f32[256,128]{1,0:T(8,128)}, f32[128,128]{0,1:T(8,128)})) %all-reduce.5.cloned.1.call-update) | async-done | bytes 196624 | tf_op jit(solution)/shard_map/psum | solution.py:32
  159.0 0.9 convert_add_fusion.1
  159.8 0.1 copy.19
  159.9 0.9 fusion.10
  160.8 11.7 %cholesky.44 = f32[128,128]{1,0:T(8,128)S(1)} custom-call(f32[128,128]{1,0:T(8,128)S(1)} %fusion.10), custom_call_target="Cholesky" | custom-call | tf_op jit(solution)/shard_map/jit(cholesky)/cholesky | solution.py:33
  172.5 0.6 compare_reduce_fusion.1
  173.2 0.7 fusion.1
  173.8 9.8 %custom-call.16 = f32[1,128,128]{1,2,0:T(8,128)S(1)} custom-call(f32[1,128,128]{2,1,0:T(8,128)S(1)} %fusion.1), custom_call_target="InvertDiagBlocksLowerTriangular" | custom-call | tf_op jit(solution)/shard_map/jit(_cho_solve)/triangular_solve | solution.py:34
  183.6 1.2 fusion.8
  184.9 0.4 convolution_convert_fusion.1
  185.3 0.8 fusion.15
  186.1 2.1 fusion.16
  188.2 1.2 copy.17
  189.5 183.2 %all-reduce.7.cloned.1.call-done = (f32[128,1024]{1,0:T(8,128)}, f32[128,128]{0,1:T(8,128)}) async-done(((f32[128,1024]{1,0:T(8,128)}, f32[128,128]{0,1:T(8,128)}), (f32[128,1024]{1,0:T(8,128)}, f32[128,128]{0,1:T(8,128)})) %all-reduce.7.cloned.1.call-update) | async-done | bytes 589840 | tf_op jit(solution)/shard_map/psum | solution.py:37
  372.7 0.9 convert_add_fusion
  373.5 0.1 copy.21
  373.6 0.9 fusion.6
  374.5 11.7 %cholesky.55 = f32[128,128]{1,0:T(8,128)S(1)} custom-call(f32[128,128]{1,0:T(8,128)S(1)} %fusion.6), custom_call_target="Cholesky" | custom-call | tf_op jit(solution)/shard_map/jit(cholesky)/cholesky | solution.py:38
  386.3 0.6 compare_reduce_fusion
  386.9 0.7 fusion.2
  387.6 9.9 %custom-call.17 = f32[1,128,128]{1,2,0:T(8,128)S(1)} custom-call(f32[1,128,128]{2,1,0:T(8,128)S(1)} %fusion.2), custom_call_target="InvertDiagBlocksLowerTriangular" | custom-call | tf_op jit(solution)/shard_map/jit(_cho_solve)/triangular_solve | solution.py:39
  397.5 1.7 fusion.4
  399.2 0.6 convolution_convert_fusion
  399.8 0.3 fusion
  400.1 21.6 %all_to_all.21 = bf16[16,64,256]{2,1,0:T(8,128)(2,1)S(1)} all-to-all(bf16[16,64,256]{2,1,0:T(8,128)(2,1)S(1)} %bitcast.50), channel_id=1, replica_groups=mesh['samp'=16,'gene'=4,'snp'=4] {'samp'}, dimensions={0} | all-to-all | bytes 1048576 | tf_op jit(solution)/shard_map/all_to_all | solution.py:44
  421.8 1.1 stack.5
  422.9 194.4 %all_to_all.22 = bf16[16,64,4096]{2,1,0:T(8,128)(2,1)S(1)} all-to-all(bf16[16,64,4096]{2,1,0:T(8,128)(2,1)S(1)} %stack.5), channel_id=1, replica_groups=mesh['samp'=16,'gene'=4,'snp'=4] {'gene','snp'}, dimensions={0} | all-to-all | bytes 16777216 | tf_op jit(solution)/shard_map/all_to_all | solution.py:14
  617.3 10.0 %multiply_convert_fusion = bf16[1024,1024]{1,0:T(8,128)(2,1)} fusion(bf16[1024,4096]{1,0:T(8,128)(2,1)S(1)} %bitcast.48, bf16[4096,1024]{1,0:T(8,128)(2,1)S(1)} %bitcast.53), kind=kOutput, calls=%fused_computation | convolution fusion | flops 8592031744 | bytes 18874368 | tf_op jit(solution)/shard_map/dot_general | solution.py:46
  (12 shorter events, 0.2 us)
Async XLA Ops:
  6.5 1.0 copy-start
  6.5 152.4 %all-reduce.5.cloned.1.call-start = ((), (), s32[]{:S(2)}) async-start(), calls=%async_computation.2 | async-start | bytes 393216 | tf_op jit(solution)/shard_map/psum | solution.py:32
  10.4 362.3 %all-reduce.7.cloned.1.call-start = ((), (), s32[]{:S(2)}) async-start(), calls=%async_computation.3 | async-start | bytes 1179648 | tf_op jit(solution)/shard_map/psum | solution.py:37
  421.8 195.5 %slice-start = ((s8[8388608]{0:T(1024)(128)(4,1)}), s8[4194304]{0:T(1024)(128)(4,1)S(1)}, s32[]{:S(2)}) async-start(s8[8388608]{0:T(1024)(128)(4,1)} %bitcast.52), calls=%async_computation.4 | async-start | bytes 8388608
  422.9 194.5 %slice-start.1 = ((s8[8388608]{0:T(1024)(128)(4,1)}), s8[4194304]{0:T(1024)(128)(4,1)S(1)}, s32[]{:S(2)}) async-start(s8[8388608]{0:T(1024)(128)(4,1)} %bitcast.52), calls=%async_computation.5 | async-start | bytes 8388608
Sparse Core Ops, SparseCore 0:
  10.5 148.4 all-reduce.4
  188.3 184.3 all-reduce.6
